TPU v7x, 32 devices: a whole 2x2x4 slice. The times are simulated.
32 devices in a mesh: region: 4 (over x, core), sector: 8 (over z, y).
Axes of the slice: x: 2, y: 2, z: 4, core: 2. Of those that a mesh axis runs over, the one named last changes fastest.
Arguments:
- start_state: bfloat16 [4, 32, 128, 4, 128], P('region', 'sector'), may hold values from -6 to 6
- left_env: bfloat16 [4, 32, 16, 128, 128], P('region', 'sector'), may hold values from -0.125 to 0.125
- right_env: bfloat16 [4, 32, 16, 128, 128], P('region', 'sector'), may hold values from -0.5 to 0.5
- mpo_tensor: bfloat16 [16, 4, 4, 16], replicated, may hold values from -0.75 to 0.75
- decay: float32 [4, 32, 128], P('region', 'sector'), may hold values from 0.15 to 1
- energy_terms: float32 [4, 32, 128], P('region', 'sector'), may hold values from -1.2 to 1.2
- live_count: int32 [4, 8], P('region', 'sector'), may hold values from 1 to 4, as said below
Outputs:
- state_out: bfloat16 [4, 32, 128, 4, 128], P('region', 'sector')
- density: float32 [4, 32, 128, 128], P('region', 'sector')
- energy: float32 [4], P('region')
Inputs may be any that keep to these rules, and one draw needn't show every extreme that they name: `live_count`: each device's live blocks fill its first slots; some device holds 4 live blocks.
All inputs are finite; a program needn't handle non-finite values.
Results may differ from a plain program's by a relative error of at most 0.0055.
The roundings to bfloat16 on the way count: a program that leaves them out, or rounds other values in their place, can miss the bound.
Values may be sent and summed in bfloat16 or wider, within the bound.
A program may use at most 64 MiB of HBM per device.

v0:
```python
import functools
import math

import jax
import jax.numpy as jnp
from jax import lax
from jax.experimental import pallas as pl
from jax.experimental.pallas import tpu as pltpu
from jax.sharding import PartitionSpec as P

DAV = 2
EPS = 1e-06
MESH = pl.DeviceIdType.MESH
F32 = jnp.float32
BF16 = jnp.bfloat16
PAD = 8


def half_rotation(y, x):
    top = jnp.maximum(jnp.abs(x), jnp.abs(y))
    safe = jnp.where(top > 0, top, 1.0)
    xn, yn = x / safe, y / safe
    h = jnp.sqrt(xn * xn + yn * yn)
    h = jnp.where(top > 0, h, 1.0)
    big = jnp.sqrt(0.5 * (h + jnp.abs(xn)) / h)
    small = jnp.abs(yn) / (2.0 * h * big)
    big = jnp.where(top > 0, big, 1.0)
    small = jnp.where(top > 0, small, 0.0)
    cos_part = jnp.where(x >= 0, big, small)
    sin_size = jnp.where(x >= 0, small, big)
    return cos_part, jnp.where(y > 0, sin_size, -sin_size)


def kernel(
    regions, sectors, start, left, right, spread, decay, energy, live,
    state_out, density, energy_out,
    left_in, left_t, right_in, right_t, planes, rows_buf, mixed,
    current, applied, search, image, decay_all, energy_all, shift, part, gathered,
    left_send, left_recv, right_sem, own_sem, pre_send, pre_recv, sum_send, sum_recv,
):
    slots, chan, blk, _ = left.shape
    phys = start.shape[1] // blk
    wide = phys * blk
    me, mine = lax.axis_index("region"), lax.axis_index("sector")
    group = 256 // (phys * chan)
    pair = 2 * group
    for n in range(slots):
        pltpu.make_async_copy(right.at[n], right_in.at[n], right_sem.at[n]).start()

    barrier = pltpu.get_barrier_semaphore()
    for k in range(1, regions):
        pl.semaphore_signal(
            barrier, 1, device_id={"region": lax.rem(me + k, regions)}, device_id_type=MESH
        )
    for k in range(1, sectors):
        pl.semaphore_signal(
            barrier, 1, device_id={"sector": lax.rem(mine + k, sectors)}, device_id_type=MESH
        )
    pl.semaphore_wait(barrier, regions + sectors - 2)

    def left_copy(n):
        return pltpu.make_async_remote_copy(
            src_ref=left.at[n], dst_ref=left_in.at[n],
            send_sem=left_send.at[n], recv_sem=left_recv.at[n],
            device_id={"region": lax.rem(me + 1, regions)}, device_id_type=MESH,
        )

    def own_copy(n):
        return pltpu.make_async_copy(left.at[n], left_in.at[n], own_sem.at[n])

    def prefix_copies(k, slot):
        to = {"region": lax.rem(me + k, regions)}
        return [
            pltpu.make_async_remote_copy(
                src_ref=src, dst_ref=dst.at[slot],
                send_sem=pre_send.at[i, k - 1], recv_sem=pre_recv.at[i, k - 1],
                device_id=to, device_id_type=MESH,
            )
            for i, (src, dst) in enumerate(((decay, decay_all), (energy, energy_all)))
        ]

    for k in range(1, regions):
        for copy in prefix_copies(k, me):
            copy.start()

    @pl.when(me < regions - 1)
    def _():
        for n in range(slots):
            left_copy(n).start()

    @pl.when(me == 0)
    def _():
        for n in range(slots):
            own_copy(n).start()

    decay_all[me] = decay[...]
    energy_all[me] = energy[...]
    for k in range(1, regions):
        for copy in prefix_copies(k, lax.rem(me + regions - k, regions)):
            copy.wait()
    offsets = jnp.zeros((slots, blk), F32)
    for p in range(regions - 1):
        offsets = jnp.where(p < me, decay_all[p] * offsets + energy_all[p], offsets)
    shift[...] = offsets

    live_slots = live[0, 0]

    def prepare_right(n):
        pltpu.make_async_copy(right.at[n], right_in.at[n], right_sem.at[n]).wait()
        pitch = blk + PAD
        for w in range(chan):
            planes[w * pitch : w * pitch + blk, :] = right_in[n, w].astype(F32).T
        for b in range(blk):
            right_t[n, b * chan : (b + 1) * chan, :] = planes[
                pl.ds(b, chan, stride=pitch), :
            ].astype(BF16)

    def prepare_left(n):
        for u in range(chan):
            left_t[n, u * blk : (u + 1) * blk, :] = left_in[n, u].T

    def sum8(value):
        return jnp.sum(value.reshape(-1, 8, value.shape[-1]), axis=0)

    def operate(n, vector, arrive):
        for j in range(blk // pair):
            rows = right_t[n, j * pair * chan : (j + 1) * pair * chan, :]
            first = jnp.dot(rows, vector, preferred_element_type=F32).astype(BF16)
            half = group * chan
            stacked = [
                jnp.concatenate(
                    [
                        first[g * half : (g + 1) * half, t * blk : (t + 1) * blk]
                        for t in range(phys)
                    ],
                    axis=0,
                )
                for g in range(2)
            ]
            second = jnp.dot(
                spread[...], jnp.concatenate(stacked, axis=1), preferred_element_type=F32
            ).astype(BF16)
            tile = group * phys
            for g in range(2):
                row = (2 * j + g) * tile
                for u in range(chan):
                    mixed[row : row + tile, u * blk : (u + 1) * blk] = second[
                        u * tile : (u + 1) * tile, g * blk : (g + 1) * blk
                    ]
        arrive()
        rows_buf[...] = jnp.dot(mixed[...], left_t[n], preferred_element_type=F32)
        return [rows_buf[pl.ds(s, blk, stride=phys), :] for s in range(phys)]

    def reduce(turn, sums):
        lines = lax.broadcasted_iota(jnp.int32, (8, blk), 0)
        tile = jnp.zeros((8, blk), F32)
        for q, total in enumerate(sums):
            tile = jnp.where(lines == q, jnp.sum(total, axis=0, keepdims=True), tile)
        part[turn] = tile
        gathered[turn, mine] = tile

        def copy_of(k, slot):
            return pltpu.make_async_remote_copy(
                src_ref=part.at[turn], dst_ref=gathered.at[turn, slot],
                send_sem=sum_send.at[turn, k - 1], recv_sem=sum_recv.at[turn, k - 1],
                device_id={"sector": lax.rem(mine + k, sectors)}, device_id_type=MESH,
            )

        for k in range(1, sectors):
            copy_of(k, mine).start()
        for k in range(1, sectors):
            copy_of(k, lax.rem(mine + sectors - k, sectors)).wait()
        total = gathered[turn, 0]
        for i in range(1, sectors):
            total = total + gathered[turn, i]
        total = jnp.broadcast_to(jnp.sum(total, axis=1, keepdims=True), (8, blk))
        return [total[q : q + 1] for q in range(len(sums))]

    zero = jnp.zeros((8, blk), F32)

    def open_slot(n, sums):
        prepare_right(n)
        alive = jnp.where(n < live_slots, 1.0, 0.0).astype(F32)
        rows_buf[...] = start[n].astype(F32)
        firsts = []
        for t in range(phys):
            first = rows_buf[pl.ds(t, blk, stride=phys), :].T * alive
            current[n, t] = first
            firsts.append(first.astype(BF16))
        offset = shift[pl.ds(n, 1)]

        def arrive():
            @pl.when(me > 0)
            def _():
                left_copy(n).wait_recv()

            @pl.when(me == 0)
            def _():
                own_copy(n).wait()

            prepare_left(n)

        results = operate(n, jnp.concatenate(firsts, axis=1), arrive)
        a, b, c = sums
        for s in range(phys):
            first = current[n, s]
            value = results[s] + offset * first
            applied[n, s] = value
            a, b, c = a + sum8(first * first), b + sum8(first * value), c + sum8(value * value)
        return a, b, c

    sums = lax.fori_loop(0, slots, open_slot, (zero, zero, zero))
    norm_sum, first_quotient, first_sq = reduce(0, sums)
    inverse = lax.rsqrt(norm_sum + EPS)
    quotient = first_quotient * inverse * inverse
    image_sq = first_sq * inverse * inverse
    weight = norm_sum / (norm_sum + EPS)
    cos_part = inverse
    sin_part = None
    for turn in range(DAV):
        resid_sq = image_sq - quotient * quotient * (2.0 - weight)
        factor = lax.rsqrt(resid_sq + EPS)

        def next_slot(n, sums, cos_part=cos_part, sin_part=sin_part, quotient=quotient, factor=factor):
            probes = []
            for t in range(phys):
                state, moved = cos_part * current[n, t], cos_part * applied[n, t]
                if sin_part is not None:
                    state = state + sin_part * search[n, t]
                    moved = moved + sin_part * image[n, t]
                current[n, t] = state
                applied[n, t] = moved
                probe = (moved - quotient * state) * factor
                search[n, t] = probe
                probes.append(probe.astype(BF16))
            results = operate(n, jnp.concatenate(probes, axis=1), lambda: None)
            offset = shift[pl.ds(n, 1)]
            a, b, c = sums
            for s in range(phys):
                value = results[s] + offset * search[n, s].astype(BF16).astype(F32)
                image[n, s] = value
                a = a + sum8(current[n, s] * value)
                b = b + sum8(applied[n, s] * value)
                c = c + sum8(value * value)
            return a, b, c

        sums = lax.fori_loop(0, slots, next_slot, (zero, zero, zero))
        along_state, along_image, search_sq = reduce(turn + 1, sums)
        curvature = factor * (along_image - quotient * along_state)
        cos_part, sin_part = half_rotation(-2.0 * resid_sq * factor, curvature - quotient)
        cross_term = factor * (image_sq - quotient * quotient)
        inner_term = factor * quotient * (1.0 - weight)
        next_quotient = (
            cos_part * cos_part * quotient
            + cos_part * sin_part * (along_state + cross_term)
            + sin_part * sin_part * curvature
        )
        next_sq = (
            cos_part * cos_part * image_sq
            + 2.0 * cos_part * sin_part * along_image
            + sin_part * sin_part * search_sq
        )
        weight = (
            cos_part * cos_part * weight
            + 2.0 * cos_part * sin_part * inner_term
            + sin_part * sin_part * resid_sq * factor * factor
        )
        quotient, image_sq = next_quotient, next_sq

    energy_out[0] = quotient[0, 0]
    scale = math.sqrt(slots * sectors * blk * phys * blk)

    def close_slot(n, carry):
        total = jnp.zeros((blk, blk), F32)
        for s in range(phys):
            state = scale * (cos_part * current[n, s] + sin_part * search[n, s])
            turned = state.T
            rows_buf[pl.ds(s, blk, stride=phys), :] = turned
            total = total + jnp.dot(
                turned.astype(BF16), state.astype(BF16), preferred_element_type=F32
            )
        state_out[n] = rows_buf[...].astype(BF16)
        density[n] = total / (phys * blk)
        return carry

    lax.fori_loop(0, slots, close_slot, 0)

    @pl.when(me < regions - 1)
    def _():
        for n in range(slots):
            left_copy(n).wait_send()


def body(regions, sectors, start_state, left_env, right_env, mpo_tensor, decay, energy_terms, live_count):
    _, slots, blk, phys, _ = start_state.shape
    chan = left_env.shape[2]
    wide = phys * blk
    group = 256 // (phys * chan)
    spread = jnp.einsum(
        "ustw,gh->ugsthw", mpo_tensor, jnp.eye(group, dtype=mpo_tensor.dtype)
    ).reshape(chan * group * phys, phys * group * chan)
    vmem = pl.BlockSpec(memory_space=pltpu.VMEM)
    hbm = pl.BlockSpec(memory_space=pl.ANY)
    smem = pl.BlockSpec(memory_space=pltpu.SMEM)
    dma = pltpu.SemaphoreType.DMA
    state = pltpu.VMEM((slots, phys, blk, blk), F32)
    outs = pl.pallas_call(
        functools.partial(kernel, regions, sectors),
        out_shape=(
            jax.ShapeDtypeStruct((slots, wide, blk), BF16),
            jax.ShapeDtypeStruct((slots, blk, blk), F32),
            jax.ShapeDtypeStruct((1,), F32),
        ),
        in_specs=[vmem, hbm, hbm, vmem, vmem, vmem, smem],
        out_specs=(vmem, vmem, smem),
        scratch_shapes=[
            pltpu.VMEM((slots, chan, blk, blk), BF16),
            pltpu.VMEM((slots, chan * blk, blk), BF16),
            pltpu.VMEM((slots, chan, blk, blk), BF16),
            pltpu.VMEM((slots, chan * blk, blk), BF16),
            pltpu.VMEM((chan * (blk + PAD), blk), F32),
            pltpu.VMEM((wide, blk), F32),
            pltpu.VMEM((wide, chan * blk), BF16),
            state, state, state, state,
            pltpu.VMEM((regions, slots, blk), F32),
            pltpu.VMEM((regions, slots, blk), F32),
            pltpu.VMEM((slots, blk), F32),
            pltpu.VMEM((DAV + 1, 8, blk), F32),
            pltpu.VMEM((DAV + 1, sectors, 8, blk), F32),
            dma((slots,)), dma((slots,)), dma((slots,)), dma((slots,)),
            dma((2, regions)), dma((2, regions)),
            dma((DAV + 1, sectors)), dma((DAV + 1, sectors)),
        ],
        compiler_params=pltpu.CompilerParams(collective_id=0, has_side_effects=True),
    )(
        start_state.reshape(slots, wide, blk), left_env[0], right_env[0], spread,
        decay[0], energy_terms[0], live_count,
    )
    return (
        outs[0].reshape(start_state.shape),
        outs[1].reshape(1, slots, blk, blk),
        outs[2],
    )


def solution(mesh):
    in_specs = (
        P("region", "sector", None, None, None),
        P("region", "sector", None, None, None),
        P("region", "sector", None, None, None),
        P(),
        P("region", "sector", None),
        P("region", "sector", None),
        P("region", "sector"),
    )
    out_specs = (
        P("region", "sector", None, None, None),
        P("region", "sector", None, None),
        P("region"),
    )
    step = functools.partial(body, mesh.shape["region"], mesh.shape["sector"])
    return jax.shard_map(step, mesh=mesh, in_specs=in_specs, out_specs=out_specs, check_vma=False)
```

profile of v0, /device:TPU:2, one launch (start us, length us, event | category | flops | bytes accessed | tf_op | source)
XLA Modules:
  0.0 72.0 jit_solution(12718188883018545343)
XLA Ops:
  1.3 1.3 %multiply_bitcast_fusion = bf16[16,4,4,4,4,16]{5,4,3,2,1,0:T(4,128)(2,1)S(1)} fusion(bf16[16,4,4,16]{3,2,1,0:T(4,128)(2,1)} %param.10, bf16[4,4]{1,0:T(4,128)(2,1)S(1)} %fusion), kind=kLoop, calls=%fused_computation | loop fusion | flops 65536 | bytes 139296 | tf_op jit(solution)/shard_map/ustw,gh->ugsthw/transpose | solution.py:299
  2.6 1.7 %reshape.19.spread = bf16[256,256]{1,0:T(8,128)(2,1)} reshape(bf16[16,4,4,4,4,16]{5,4,3,2,1,0:T(4,128)(2,1)S(1)} %multiply_bitcast_fusion) | data formatting | bytes 262144 | tf_op jit(solution)/shard_map/reshape | solution.py:301
  4.2 62.4 %shard_map.94 = (bf16[4,512,128]{2,1,0:T(8,128)(2,1)}, f32[4,128,128]{2,1,0:T(8,128)}, f32[1]{0:T(128)}) custom-call(bf16[4,512,128]{2,1,0:T(8,128)(2,1)} %bitcast.11, bf16[4,16,128,128]{3,2,1,0:T(8,128)(2,1)} %bitcast.9, bf16[4,16,128,128]{3,2,1,0:T(8,128)(2,1)} %bitcast.10, bf16[256,256]{1,0:T(8,128)(2,1)} %reshape.19.spread, f32[4,128]{1,0:T(4,128)} %bitcast.14, ...), custom_call_target="tpu_custom_call" | custom-call | tf_op jit(solution)/shard_map/pallas_call | solution.py:307
  66.6 2.0 %copy.14 = bf16[1,4,128,4,128]{4,3,2,1,0:T(4,128)(2,1)} copy(bf16[1,4,128,4,128]{4,3,2,1,0:T(4,128)(2,1)} %bitcast.12) | data formatting | bytes 1048576
  68.7 1.7 %copy.15 = f32[1,4,128,128]{3,2,1,0:T(8,128)} copy(f32[1,4,128,128]{3,2,1,0:T(8,128)} %bitcast.13) | data formatting | bytes 524288
  (1 shorter events, 0.0 us)
where the time goes:
time: 72.3 us; the launch traced here: 72 us
  Pallas kernels  62.4 us (86%)
  local copies, waits for them, and re-layouts  5.34 us (7%)
  between operations  2.97 us (4%)
  other arithmetic  1.31 us (2%)
    pallas_call x1, Pallas kernels, body(): pl.pallas_call(functools.partial(kernel, regions, sectors), out_shape=(ja...  62.4 us
    unnamed x2, local copies, waits for them, and re-layouts  3.68 us
    reshape x1, local copies, waits for them, and re-layouts, body(): spread = jnp.einsum('ustw,gh->ugsthw', mpo_tensor, jnp.eye(group, dtype=m...  1.65 us

commit v1 on v0

--- a/solution.py
+++ b/solution.py
@@ -32,11 +32,11 @@
 
 
 def kernel(
-    regions, sectors, start, left, right, spread, decay, energy, live,
-    state_out, density, energy_out,
-    left_in, left_t, right_in, right_t, planes, rows_buf, mixed,
+    regions, sectors, start, left, right, operator, decay, energy, live,
+    state_out, energy_out,
+    start_in, left_in, left_t, right_in, right_t, planes, rows_buf, mixed, lines, spread,
     current, applied, search, image, decay_all, energy_all, shift, part, gathered,
-    left_send, left_recv, right_sem, own_sem, pre_send, pre_recv, sum_send, sum_recv,
+    left_send, left_recv, right_sem, own_sem, start_sem, pre_send, pre_recv, sum_send, sum_recv,
 ):
     slots, chan, blk, _ = left.shape
     phys = start.shape[1] // blk
@@ -46,6 +46,7 @@
     pair = 2 * group
     for n in range(slots):
         pltpu.make_async_copy(right.at[n], right_in.at[n], right_sem.at[n]).start()
+        pltpu.make_async_copy(start.at[n], start_in.at[n], start_sem.at[n]).start()
 
     barrier = pltpu.get_barrier_semaphore()
     for k in range(1, regions):
@@ -105,6 +106,31 @@
 
     live_slots = live[0, 0]
 
+    side = group * phys * chan
+    lines[...] = operator[...].astype(F32)
+
+    def where_one(test):
+        return jnp.where(test, 1.0, 0.0).astype(BF16)
+
+    def grid_of(shape):
+        return [lax.broadcasted_iota(jnp.int32, shape, i) for i in range(2)]
+
+    r, c = grid_of((side, chan * phys))
+    pick_row = where_one((r // (group * phys) == c // phys) & (r % phys == c % phys))
+    r, c = grid_of((chan, side))
+    total = jnp.zeros((side, side), F32)
+    for t in range(phys):
+        tall = jnp.dot(
+            pick_row,
+            lines[pl.ds(t, chan * phys, stride=phys), :].astype(BF16),
+            preferred_element_type=F32,
+        ).astype(BF16)
+        pick_column = where_one((c // (group * chan) == t) & (c % chan == r))
+        total = total + jnp.dot(tall, pick_column, preferred_element_type=F32)
+    r, c = grid_of((side, side))
+    same = (r // phys) % group == (c // chan) % group
+    spread[...] = jnp.where(same, total, 0.0).astype(BF16)
+
     def prepare_right(n):
         pltpu.make_async_copy(right.at[n], right_in.at[n], right_sem.at[n]).wait()
         pitch = blk + PAD
@@ -122,11 +148,11 @@
     def sum8(value):
         return jnp.sum(value.reshape(-1, 8, value.shape[-1]), axis=0)
 
-    def operate(n, vector, arrive):
+    def operate(n, slot, vector, arrive):
+        half = group * chan
         for j in range(blk // pair):
             rows = right_t[n, j * pair * chan : (j + 1) * pair * chan, :]
             first = jnp.dot(rows, vector, preferred_element_type=F32).astype(BF16)
-            half = group * chan
             stacked = [
                 jnp.concatenate(
                     [
@@ -144,18 +170,18 @@
             for g in range(2):
                 row = (2 * j + g) * tile
                 for u in range(chan):
-                    mixed[row : row + tile, u * blk : (u + 1) * blk] = second[
+                    mixed[slot, row : row + tile, u * blk : (u + 1) * blk] = second[
                         u * tile : (u + 1) * tile, g * blk : (g + 1) * blk
                     ]
         arrive()
-        rows_buf[...] = jnp.dot(mixed[...], left_t[n], preferred_element_type=F32)
-        return [rows_buf[pl.ds(s, blk, stride=phys), :] for s in range(phys)]
+        rows_buf[slot] = jnp.dot(mixed[slot], left_t[n], preferred_element_type=F32)
+        return [rows_buf[slot, pl.ds(s, blk, stride=phys), :] for s in range(phys)]
 
     def reduce(turn, sums):
-        lines = lax.broadcasted_iota(jnp.int32, (8, blk), 0)
+        line = lax.broadcasted_iota(jnp.int32, (8, blk), 0)
         tile = jnp.zeros((8, blk), F32)
         for q, total in enumerate(sums):
-            tile = jnp.where(lines == q, jnp.sum(total, axis=0, keepdims=True), tile)
+            tile = jnp.where(line == q, jnp.sum(total, axis=0, keepdims=True), tile)
         part[turn] = tile
         gathered[turn, mine] = tile
 
@@ -181,10 +207,11 @@
     def open_slot(n, sums):
         prepare_right(n)
         alive = jnp.where(n < live_slots, 1.0, 0.0).astype(F32)
-        rows_buf[...] = start[n].astype(F32)
+        pltpu.make_async_copy(start.at[n], start_in.at[n], start_sem.at[n]).wait()
+        rows_buf[0] = start_in[n].astype(F32)
         firsts = []
         for t in range(phys):
-            first = rows_buf[pl.ds(t, blk, stride=phys), :].T * alive
+            first = rows_buf[0, pl.ds(t, blk, stride=phys), :].T * alive
             current[n, t] = first
             firsts.append(first.astype(BF16))
         offset = shift[pl.ds(n, 1)]
@@ -200,7 +227,7 @@
 
             prepare_left(n)
 
-        results = operate(n, jnp.concatenate(firsts, axis=1), arrive)
+        results = operate(n, 0, jnp.concatenate(firsts, axis=1), arrive)
         a, b, c = sums
         for s in range(phys):
             first = current[n, s]
@@ -233,7 +260,7 @@
                 probe = (moved - quotient * state) * factor
                 search[n, t] = probe
                 probes.append(probe.astype(BF16))
-            results = operate(n, jnp.concatenate(probes, axis=1), lambda: None)
+            results = operate(n, 0, jnp.concatenate(probes, axis=1), lambda: None)
             offset = shift[pl.ds(n, 1)]
             a, b, c = sums
             for s in range(phys):
@@ -270,25 +297,26 @@
     energy_out[0] = quotient[0, 0]
     scale = math.sqrt(slots * sectors * blk * phys * blk)
 
-    def close_slot(n, carry):
-        total = jnp.zeros((blk, blk), F32)
-        for s in range(phys):
-            state = scale * (cos_part * current[n, s] + sin_part * search[n, s])
-            turned = state.T
-            rows_buf[pl.ds(s, blk, stride=phys), :] = turned
-            total = total + jnp.dot(
-                turned.astype(BF16), state.astype(BF16), preferred_element_type=F32
-            )
-        state_out[n] = rows_buf[...].astype(BF16)
-        density[n] = total / (phys * blk)
-        return carry
-
-    lax.fori_loop(0, slots, close_slot, 0)
+    for n in range(slots):
+        for t in range(phys):
+            state = cos_part * current[n, t] + sin_part * search[n, t]
+            state_out[n, t] = (scale * state).astype(BF16)
 
     @pl.when(me < regions - 1)
     def _():
         for n in range(slots):
             left_copy(n).wait_send()
+
+
+def finish(state, out, density, rows_buf):
+    _, phys, blk, _ = state.shape
+    total = jnp.zeros((blk, blk), F32)
+    for s in range(phys):
+        turned = state[0, s].T
+        rows_buf[pl.ds(s, blk, stride=phys), :] = turned.astype(F32)
+        total = total + jnp.dot(turned, state[0, s], preferred_element_type=F32)
+    out[0] = rows_buf[...].astype(BF16)
+    density[0] = total / (phys * blk)
 
 
 def body(regions, sectors, start_state, left_env, right_env, mpo_tensor, decay, energy_terms, live_count):
@@ -296,9 +324,6 @@
     chan = left_env.shape[2]
     wide = phys * blk
     group = 256 // (phys * chan)
-    spread = jnp.einsum(
-        "ustw,gh->ugsthw", mpo_tensor, jnp.eye(group, dtype=mpo_tensor.dtype)
-    ).reshape(chan * group * phys, phys * group * chan)
     vmem = pl.BlockSpec(memory_space=pltpu.VMEM)
     hbm = pl.BlockSpec(memory_space=pl.ANY)
     smem = pl.BlockSpec(memory_space=pltpu.SMEM)
@@ -307,39 +332,56 @@
     outs = pl.pallas_call(
         functools.partial(kernel, regions, sectors),
         out_shape=(
-            jax.ShapeDtypeStruct((slots, wide, blk), BF16),
-            jax.ShapeDtypeStruct((slots, blk, blk), F32),
+            jax.ShapeDtypeStruct((slots, phys, blk, blk), BF16),
             jax.ShapeDtypeStruct((1,), F32),
         ),
-        in_specs=[vmem, hbm, hbm, vmem, vmem, vmem, smem],
-        out_specs=(vmem, vmem, smem),
+        in_specs=[hbm, hbm, hbm, vmem, vmem, vmem, smem],
+        out_specs=(vmem, smem),
         scratch_shapes=[
+            pltpu.VMEM((slots, wide, blk), BF16),
             pltpu.VMEM((slots, chan, blk, blk), BF16),
             pltpu.VMEM((slots, chan * blk, blk), BF16),
             pltpu.VMEM((slots, chan, blk, blk), BF16),
             pltpu.VMEM((slots, chan * blk, blk), BF16),
             pltpu.VMEM((chan * (blk + PAD), blk), F32),
-            pltpu.VMEM((wide, blk), F32),
-            pltpu.VMEM((wide, chan * blk), BF16),
+            pltpu.VMEM((2, wide, blk), F32),
+            pltpu.VMEM((2, wide, chan * blk), BF16),
+            pltpu.VMEM((chan * phys * phys, chan), F32),
+            pltpu.VMEM((group * phys * chan, group * phys * chan), BF16),
             state, state, state, state,
             pltpu.VMEM((regions, slots, blk), F32),
             pltpu.VMEM((regions, slots, blk), F32),
             pltpu.VMEM((slots, blk), F32),
             pltpu.VMEM((DAV + 1, 8, blk), F32),
             pltpu.VMEM((DAV + 1, sectors, 8, blk), F32),
-            dma((slots,)), dma((slots,)), dma((slots,)), dma((slots,)),
+            dma((slots,)), dma((slots,)), dma((slots,)), dma((slots,)), dma((slots,)),
             dma((2, regions)), dma((2, regions)),
             dma((DAV + 1, sectors)), dma((DAV + 1, sectors)),
         ],
         compiler_params=pltpu.CompilerParams(collective_id=0, has_side_effects=True),
     )(
-        start_state.reshape(slots, wide, blk), left_env[0], right_env[0], spread,
+        start_state.reshape(slots, wide, blk), left_env[0], right_env[0],
+        mpo_tensor.reshape(chan * phys * phys, chan),
         decay[0], energy_terms[0], live_count,
     )
+    state_out, density = pl.pallas_call(
+        finish,
+        grid=(slots,),
+        out_shape=(
+            jax.ShapeDtypeStruct((slots, wide, blk), BF16),
+            jax.ShapeDtypeStruct((slots, blk, blk), F32),
+        ),
+        in_specs=[pl.BlockSpec((1, phys, blk, blk), lambda n: (n, 0, 0, 0))],
+        out_specs=(
+            pl.BlockSpec((1, wide, blk), lambda n: (n, 0, 0)),
+            pl.BlockSpec((1, blk, blk), lambda n: (n, 0, 0)),
+        ),
+        scratch_shapes=[pltpu.VMEM((wide, blk), F32)],
+    )(outs[0])
     return (
-        outs[0].reshape(start_state.shape),
-        outs[1].reshape(1, slots, blk, blk),
-        outs[2],
+        state_out.reshape(start_state.shape),
+        density.reshape(1, slots, blk, blk),
+        outs[1],
     )
 
 

time: 72.3 us -> 68.1 us (0.942)
  local copies, waits for them, and re-layouts: 5.34 us -> 0 us
  Pallas kernels: 62.4 us -> 64.8 us
  other arithmetic: 1.31 us -> 0 us
    unnamed x2 -> x0, local copies, waits for them, and re-layouts: 3.68 us -> none
    pallas_call x0 -> x1, Pallas kernels: none -> 3.54 us  [body(): pl.pallas_call(finish, grid=(slots,), out_shape=(jax.ShapeDtypeStruct((sl...]
    reshape x1 -> x0, local copies, waits for them, and re-layouts: 1.65 us -> none  [body(): spread = jnp.einsum('ustw,gh->ugsthw', mpo_tensor, jnp.eye(group, dtype=m...]
    transpose x1 -> x0, other arithmetic: 1.3 us -> none  [body(): jnp.einsum('ustw,gh->ugsthw', mpo_tensor, jnp.eye(group, dtype=mpo_tensor...]
    pallas_call x1, Pallas kernels: 62.4 us -> 61.3 us  [body(): pl.pallas_call(functools.partial(kernel, regions, sectors), out_shape=(ja...]
where the time goes in v1:
time: 68.1 us; the launch traced here: 67.9 us
  Pallas kernels  64.8 us (95%)
  between operations  3.05 us (4%)
    pallas_call x1, Pallas kernels, body(): pl.pallas_call(functools.partial(kernel, regions, sectors), out_shape=(ja...  61.3 us
    pallas_call x1, Pallas kernels, body(): pl.pallas_call(finish, grid=(slots,), out_shape=(jax.ShapeDtypeStruct((sl...  3.54 us

profile of v1, /device:TPU:2, one launch (start us, length us, event | category | flops | bytes accessed | tf_op | source)
XLA Modules:
  0.0 67.9 jit_solution(14262799968873228830)
XLA Ops:
  1.3 61.3 %shard_map.94 = (bf16[4,4,128,128]{3,2,1,0:T(8,128)(2,1)}, f32[1]{0:T(128)}) custom-call(bf16[4,512,128]{2,1,0:T(8,128)(2,1)} %bitcast.10, bf16[4,16,128,128]{3,2,1,0:T(8,128)(2,1)} %bitcast.8, bf16[4,16,128,128]{3,2,1,0:T(8,128)(2,1)} %bitcast.9, bf16[256,16]{1,0:T(8,128)(2,1)} %bitcast.11, f32[4,128]{1,0:T(4,128)} %bitcast.12, f32[4,128]{1,0:T(4,128)} %bitcast.13, ...), custom_call_target="tpu_custom_call" | custom-call | tf_op jit(solution)/shard_map/pallas_call | solution.py:332
  62.6 3.5 %shard_map.95 = (bf16[4,512,128]{2,1,0:T(8,128)(2,1)}, f32[4,128,128]{2,1,0:T(8,128)}) custom-call(bf16[4,4,128,128]{3,2,1,0:T(8,128)(2,1)} %get-tuple-element.7.state), custom_call_target="tpu_custom_call" | custom-call | tf_op jit(solution)/shard_map/pallas_call | solution.py:367

commit v2 on v1

--- a/solution.py
+++ b/solution.py
@@ -104,7 +104,7 @@
         offsets = jnp.where(p < me, decay_all[p] * offsets + energy_all[p], offsets)
     shift[...] = offsets
 
-    live_slots = live[0, 0]
+    live_slots = live[...]
 
     side = group * phys * chan
     lines[...] = operator[...].astype(F32)
@@ -206,7 +206,7 @@
 
     def open_slot(n, sums):
         prepare_right(n)
-        alive = jnp.where(n < live_slots, 1.0, 0.0).astype(F32)
+        alive = jnp.broadcast_to(jnp.where(n < live_slots, 1.0, 0.0), (1, blk)).astype(F32)
         pltpu.make_async_copy(start.at[n], start_in.at[n], start_sem.at[n]).wait()
         rows_buf[0] = start_in[n].astype(F32)
         firsts = []
@@ -294,7 +294,7 @@
         )
         quotient, image_sq = next_quotient, next_sq
 
-    energy_out[0] = quotient[0, 0]
+    energy_out[...] = jnp.broadcast_to(quotient, (8, blk))
     scale = math.sqrt(slots * sectors * blk * phys * blk)
 
     for n in range(slots):
@@ -308,15 +308,23 @@
             left_copy(n).wait_send()
 
 
-def finish(state, out, density, rows_buf):
-    _, phys, blk, _ = state.shape
-    total = jnp.zeros((blk, blk), F32)
-    for s in range(phys):
-        turned = state[0, s].T
-        rows_buf[pl.ds(s, blk, stride=phys), :] = turned.astype(F32)
-        total = total + jnp.dot(turned, state[0, s], preferred_element_type=F32)
-    out[0] = rows_buf[...].astype(BF16)
-    density[0] = total / (phys * blk)
+def finish(state, energy, out, density, energy_out, rows_buf, out_buf, density_buf, sems):
+    slots, phys, blk, _ = state.shape
+    copies = []
+    for n in range(slots):
+        total = jnp.zeros((blk, blk), F32)
+        for s in range(phys):
+            turned = state[n, s].T
+            rows_buf[n, pl.ds(s, blk, stride=phys), :] = turned.astype(F32)
+            total = total + jnp.dot(turned, state[n, s], preferred_element_type=F32)
+        out_buf[n] = rows_buf[n].astype(BF16)
+        density_buf[n] = total / (phys * blk)
+        for i, (src, dst) in enumerate(((out_buf, out), (density_buf, density))):
+            copies.append(pltpu.make_async_copy(src.at[n], dst.at[n], sems.at[i, n]))
+            copies[-1].start()
+    energy_out[0] = energy[0, 0]
+    for copy in copies:
+        copy.wait()
 
 
 def body(regions, sectors, start_state, left_env, right_env, mpo_tensor, decay, energy_terms, live_count):
@@ -333,10 +341,10 @@
         functools.partial(kernel, regions, sectors),
         out_shape=(
             jax.ShapeDtypeStruct((slots, phys, blk, blk), BF16),
-            jax.ShapeDtypeStruct((1,), F32),
+            jax.ShapeDtypeStruct((8, blk), F32),
         ),
-        in_specs=[hbm, hbm, hbm, vmem, vmem, vmem, smem],
-        out_specs=(vmem, smem),
+        in_specs=[hbm, hbm, hbm, vmem, vmem, vmem, vmem],
+        out_specs=(vmem, vmem),
         scratch_shapes=[
             pltpu.VMEM((slots, wide, blk), BF16),
             pltpu.VMEM((slots, chan, blk, blk), BF16),
@@ -364,24 +372,26 @@
         mpo_tensor.reshape(chan * phys * phys, chan),
         decay[0], energy_terms[0], live_count,
     )
-    state_out, density = pl.pallas_call(
+    state_out, density, energy = pl.pallas_call(
         finish,
-        grid=(slots,),
         out_shape=(
             jax.ShapeDtypeStruct((slots, wide, blk), BF16),
             jax.ShapeDtypeStruct((slots, blk, blk), F32),
+            jax.ShapeDtypeStruct((1,), F32),
         ),
-        in_specs=[pl.BlockSpec((1, phys, blk, blk), lambda n: (n, 0, 0, 0))],
-        out_specs=(
-            pl.BlockSpec((1, wide, blk), lambda n: (n, 0, 0)),
-            pl.BlockSpec((1, blk, blk), lambda n: (n, 0, 0)),
-        ),
-        scratch_shapes=[pltpu.VMEM((wide, blk), F32)],
-    )(outs[0])
+        in_specs=[vmem, vmem],
+        out_specs=(hbm, hbm, smem),
+        scratch_shapes=[
+            pltpu.VMEM((slots, wide, blk), F32),
+            pltpu.VMEM((slots, wide, blk), BF16),
+            pltpu.VMEM((slots, blk, blk), F32),
+            dma((2, slots)),
+        ],
+    )(*outs)
     return (
         state_out.reshape(start_state.shape),
         density.reshape(1, slots, blk, blk),
-        outs[1],
+        energy,
     )
 
 

time: 68.1 us -> 65.3 us (0.959)
  between operations: 3.05 us -> 1.29 us
  Pallas kernels: 64.8 us -> 63.8 us
    pallas_call x1, Pallas kernels: 3.54 us -> 2.73 us  [body(): pl.pallas_call(finish, out_shape=(jax.ShapeDtypeStruct((slots, wide, blk)...]
where the time goes in v2:
time: 65.3 us; the launch traced here: 65.1 us
  Pallas kernels  63.8 us (98%)
  between operations  1.29 us (2%)
    pallas_call x1, Pallas kernels, body(): pl.pallas_call(functools.partial(kernel, regions, sectors), out_shape=(ja...  61.1 us
    pallas_call x1, Pallas kernels, body(): pl.pallas_call(finish, out_shape=(jax.ShapeDtypeStruct((slots, wide, blk)...  2.73 us

profile of v2, /device:TPU:2, one launch (start us, length us, event | category | flops | bytes accessed | tf_op | source)
XLA Modules:
  0.0 65.1 jit_solution(589796659616348689)
XLA Ops:
  1.3 61.1 %shard_map.94 = (bf16[4,4,128,128]{3,2,1,0:T(8,128)(2,1)}, f32[8,128]{1,0:T(8,128)}) custom-call(bf16[4,512,128]{2,1,0:T(8,128)(2,1)} %bitcast.10, bf16[4,16,128,128]{3,2,1,0:T(8,128)(2,1)} %bitcast.8, bf16[4,16,128,128]{3,2,1,0:T(8,128)(2,1)} %bitcast.9, bf16[256,16]{1,0:T(8,128)(2,1)} %bitcast.11, f32[4,128]{1,0:T(4,128)} %bitcast.12, f32[4,128]{1,0:T(4,128)} %bitcast.13, ...), custom_call_target="tpu_custom_call" | custom-call | tf_op jit(solution)/shard_map/pallas_call | solution.py:340
  62.4 2.7 %shard_map.95 = (bf16[4,512,128]{2,1,0:T(8,128)(2,1)}, f32[4,128,128]{2,1,0:T(8,128)}, f32[1]{0:T(128)}) custom-call(bf16[4,4,128,128]{3,2,1,0:T(8,128)(2,1)} %get-tuple-element.8.state, f32[8,128]{1,0:T(8,128)} %get-tuple-element.9.energy), custom_call_target="tpu_custom_call" | custom-call | tf_op jit(solution)/shard_map/pallas_call | solution.py:375
